TPU v7x, 32 devices: a whole 2x2x4 slice. The times are simulated.
32 devices in a mesh: expert: 8 (over z, x), hidden: 4 (over y, core).
Axes of the slice: x: 2, y: 2, z: 4, core: 2. Of those that a mesh axis runs over, the one named last changes fastest.
Arguments:
- tokens: bfloat16 [16384, 768], P(('expert', 'hidden')), may hold values from -6 to 6
- doc_lengths: int32 [8, 3], P('expert'), may hold values from 1 to 1024, 2048 in all within a row
- expert_ids: int32 [16384, 2], P(('expert', 'hidden')), may hold values from 0 to 7, all different within a row; in each aligned block of 512 rows (0 to 511, 512 to 1023, ...) at most 160 rows name the same one
- gain_one: float32 [768], replicated, may hold values from 0.5 to 1.5
- shift_one: float32 [768], replicated, may hold values from -1.25 to 1.25
- w_query: bfloat16 [768, 768], replicated, may hold values from -0.21875 to 0.21875
- w_key: bfloat16 [768, 768], replicated, may hold values from -0.21875 to 0.21875
- w_value: bfloat16 [768, 768], replicated, may hold values from -0.21875 to 0.21875
- w_out: bfloat16 [768, 768], replicated, may hold values from -3.5 to 3.5
- gain_two: float32 [768], replicated, may hold values from 0.5 to 1.5
- shift_two: float32 [768], replicated, may hold values from -1.25 to 1.25
- w_router: bfloat16 [768, 8], replicated, may hold values from -0.21875 to 0.21875
- w_up: bfloat16 [8, 768, 3072], P('expert', None, 'hidden'), may hold values from -0.21875 to 0.21875
- w_down: bfloat16 [8, 3072, 768], P('expert', 'hidden'), may hold values from -0.109375 to 0.109375
- out_grad: bfloat16 [16384, 768], P(('expert', 'hidden')), may hold values from -6 to 6
Outputs:
- output: bfloat16 [16384, 768], P(('expert', 'hidden'))
- input_grad: bfloat16 [16384, 768], P(('expert', 'hidden'))
- gain_one_grad: float32 [768], replicated
- shift_one_grad: float32 [768], replicated
- w_query_grad: float32 [768, 768], replicated
- w_key_grad: float32 [768, 768], replicated
- w_value_grad: float32 [768, 768], replicated
- w_out_grad: float32 [768, 768], replicated
- gain_two_grad: float32 [768], replicated
- shift_two_grad: float32 [768], replicated
- w_router_grad: float32 [768, 8], replicated
- w_up_grad: float32 [8, 768, 3072], P('expert', None, 'hidden')
- w_down_grad: float32 [8, 3072, 768], P('expert', 'hidden')
- load: float32 [8], replicated
Inputs may be any that keep to these rules, and one draw needn't show every extreme that they name: `doc_lengths`: the lengths of a group's documents, in order; they sum to 2048 and the longest in every group is 1024. `expert_ids`: each token names 2 different experts; among the 512 tokens of one device no expert is named more than 160 times, and in every draw some expert is named exactly 160 times by one device.
All inputs are finite; a program needn't handle non-finite values.
Results may differ from a plain program's by a relative error of at most 0.019.
Values may be sent and summed in bfloat16 or wider, within the bound.
A program may use at most 192 MiB of HBM per device.

v0:
```python
from functools import partial
import jax
import jax.numpy as jnp
from jax import lax
from jax.sharding import PartitionSpec as P

HEADS = 12
HEAD_DIM = 64
EPSILON = 1e-05
SCALE = 0.125
MASKED = -1e30
EXACT = lax.Precision.HIGHEST


def product(left, right):
    return jnp.dot(left, right, preferred_element_type=jnp.float32)


def contract(left, right, left_axis, right_axis):
    return lax.dot_general(
        left, right, (((left_axis,), (right_axis,)), ((), ())), preferred_element_type=jnp.float32
    )


def norm_parts(values):
    row_mean = jnp.mean(values, axis=-1, keepdims=True)
    centred = values - row_mean
    inverse = lax.rsqrt(jnp.mean(centred * centred, axis=-1, keepdims=True) + EPSILON)
    return (centred * inverse, inverse)


def norm_back(grad_out, normed, inverse, gain):
    grad_normed = grad_out * gain
    first_mean = jnp.mean(grad_normed, axis=-1, keepdims=True)
    second_mean = jnp.mean(grad_normed * normed, axis=-1, keepdims=True)
    return inverse * (grad_normed - first_mean - normed * second_mean)


def gelu_back(pre_act, grad_hidden):
    unused, pull = jax.vjp(partial(jax.nn.gelu, approximate=True), pre_act)
    return pull(grad_hidden)[0]


def split_heads(array):
    return array.reshape(array.shape[0], HEADS, HEAD_DIM).transpose(1, 0, 2)


def join_heads(array):
    return array.transpose(1, 0, 2).reshape(array.shape[1], HEADS * HEAD_DIM)


def shards(
    tokens,
    doc_lengths,
    expert_ids,
    gain_one,
    shift_one,
    w_query,
    w_key,
    w_value,
    w_out,
    gain_two,
    shift_two,
    w_router,
    w_up,
    w_down,
    out_grad,
):
    row_count = tokens.shape[0]
    model_width = tokens.shape[1]
    top_count = expert_ids.shape[1]
    experts = lax.axis_size("expert") * w_up.shape[0]
    capacity = max(2, row_count * top_count * 5 // (4 * experts))
    input_float = tokens.astype(jnp.float32)
    normed_one, inverse_one = norm_parts(input_float)
    h_one = (normed_one * gain_one + shift_one).astype(jnp.bfloat16)
    queries = product(h_one, w_query).astype(jnp.bfloat16)
    key_proj = product(h_one, w_key).astype(jnp.bfloat16)
    value_proj = product(h_one, w_value).astype(jnp.bfloat16)
    all_keys, all_values = (
        lax.all_gather(key_proj, "hidden", axis=0, tiled=True),
        lax.all_gather(value_proj, "hidden", axis=0, tiled=True),
    )
    key_count = all_keys.shape[0]
    doc_ends = jnp.cumsum(doc_lengths[0])
    query_pos = lax.axis_index("hidden") * row_count + jnp.arange(row_count, dtype=jnp.int32)
    key_pos = jnp.arange(key_count, dtype=jnp.int32)
    query_doc = jnp.sum((query_pos[:, None] >= doc_ends[None, :]).astype(jnp.int32), axis=1)
    key_doc = jnp.sum((key_pos[:, None] >= doc_ends[None, :]).astype(jnp.int32), axis=1)
    allowed = (query_doc[:, None] == key_doc[None, :]) & (key_pos[None, :] <= query_pos[:, None])

    def head_forward(pieces):
        q_head, k_head, v_head = pieces
        scores = jnp.where(allowed, contract(q_head, k_head, 1, 1) * SCALE, MASKED)
        top_score = jnp.max(scores, axis=1, keepdims=True)
        expd = jnp.exp(scores - top_score)
        row_total = jnp.sum(expd, axis=1, keepdims=True)
        weights = (expd / row_total).astype(jnp.bfloat16)
        return (product(weights, v_head), (top_score + jnp.log(row_total))[:, 0])

    mixture, log_total = lax.map(
        head_forward, (split_heads(queries), split_heads(all_keys), split_heads(all_values))
    )
    attended = join_heads(mixture).astype(jnp.bfloat16)
    residual = input_float + product(attended, w_out)
    normed_two, inverse_two = norm_parts(residual)
    h_two = (normed_two * gain_two + shift_two).astype(jnp.bfloat16)
    h_two_float = h_two.astype(jnp.float32)
    router_float = w_router.astype(jnp.float32)
    logits = jnp.dot(h_two_float, router_float, precision=EXACT)
    choose_table = (
        expert_ids[:, :, None] == jnp.arange(experts, dtype=jnp.int32)[None, None, :]
    ).astype(jnp.float32)
    chosen = jnp.sum(choose_table * logits[:, None, :], axis=2)
    gate_weights = jax.nn.softmax(chosen, axis=1)
    flat_ids = expert_ids.reshape(-1)
    onehot = choose_table.reshape(-1, experts).astype(jnp.int32)
    before = jnp.cumsum(onehot, axis=0) - onehot
    slot_index = jnp.sum(before * onehot, axis=1)
    counts = jnp.sum(choose_table, axis=(0, 1))
    outgoing = (
        jnp.zeros((experts, capacity, model_width), jnp.bfloat16)
        .at[flat_ids, slot_index]
        .set(jnp.repeat(h_two, top_count, axis=0))
    )
    slot_rows = lax.all_to_all(outgoing, "expert", split_axis=0, concat_axis=0, tiled=True).reshape(
        -1, model_width
    )
    rows_all = lax.all_gather(slot_rows, "hidden", axis=0, tiled=True)
    pre_act = product(rows_all, w_up[0])
    hidden_act = jax.nn.gelu(pre_act, approximate=True).astype(jnp.bfloat16)
    partial_sum = product(hidden_act, w_down[0])
    produced = lax.psum_scatter(
        partial_sum.astype(jnp.bfloat16), "hidden", scatter_dimension=0, tiled=True
    )
    returned = lax.all_to_all(
        produced.reshape(-1, capacity, model_width),
        "expert",
        split_axis=0,
        concat_axis=0,
        tiled=True,
    )
    returned_rows = (
        returned[flat_ids, slot_index]
        .reshape(row_count, top_count, model_width)
        .astype(jnp.float32)
    )
    expert_mix = jnp.sum(gate_weights[:, :, None] * returned_rows, axis=1)
    output = (residual + expert_mix).astype(jnp.bfloat16)
    grad_output = out_grad.astype(jnp.float32)
    grad_returned = (gate_weights[:, :, None] * grad_output[:, None, :]).astype(jnp.bfloat16)
    grad_gates = jnp.sum(returned_rows * grad_output[:, None, :], axis=2)
    grad_chosen = gate_weights * (
        grad_gates - jnp.sum(gate_weights * grad_gates, axis=1, keepdims=True)
    )
    grad_logits = jnp.sum(grad_chosen[:, :, None] * choose_table, axis=1)
    router_grad = jnp.dot(h_two_float.T, grad_logits, precision=EXACT)
    grad_h_two = jnp.dot(grad_logits, router_float.T, precision=EXACT)
    grad_outgoing = (
        jnp.zeros((experts, capacity, model_width), jnp.bfloat16)
        .at[flat_ids, slot_index]
        .set(grad_returned.reshape(-1, model_width))
    )
    grad_slots = lax.all_to_all(
        grad_outgoing, "expert", split_axis=0, concat_axis=0, tiled=True
    ).reshape(-1, model_width)
    trainable = (lax.axis_index("expert") >= experts // 2).astype(jnp.float32)
    grad_all = lax.all_gather(grad_slots, "hidden", axis=0, tiled=True)
    grad_hidden = contract(grad_all, w_down[0], 1, 1)
    down_grad = contract(hidden_act, grad_all, 0, 0)
    grad_pre = gelu_back(pre_act, grad_hidden).astype(jnp.bfloat16)
    up_grad = contract(rows_all, grad_pre, 0, 0)
    partial_in = contract(grad_pre, w_up[0], 1, 1)
    grad_in = lax.psum_scatter(
        partial_in.astype(jnp.bfloat16), "hidden", scatter_dimension=0, tiled=True
    )
    up_grad = up_grad[None] * trainable
    down_grad = down_grad[None] * trainable
    grad_back = lax.all_to_all(
        grad_in.reshape(-1, capacity, model_width),
        "expert",
        split_axis=0,
        concat_axis=0,
        tiled=True,
    )
    grad_h_two = grad_h_two + jnp.sum(
        grad_back[flat_ids, slot_index]
        .reshape(row_count, top_count, model_width)
        .astype(jnp.float32),
        axis=1,
    )
    gain_two_grad = jnp.sum(grad_h_two * normed_two, axis=0)
    shift_two_grad = jnp.sum(grad_h_two, axis=0)
    grad_residual = grad_output + norm_back(grad_h_two, normed_two, inverse_two, gain_two)
    grad_branch = grad_residual.astype(jnp.bfloat16)
    out_proj_grad = contract(attended, grad_branch, 0, 0)
    grad_attended = contract(grad_branch, w_out, 1, 1).astype(jnp.bfloat16)
    back_keys, back_values = (all_keys, all_values)

    def head_backward(pieces):
        q_head, k_head, v_head, g_head, head_total = pieces
        scores = jnp.where(allowed, contract(q_head, k_head, 1, 1) * SCALE, MASKED)
        weights = jnp.exp(scores - head_total[:, None])
        grad_weights = contract(g_head, v_head, 1, 1)
        grad_scores = (
            weights * (grad_weights - jnp.sum(weights * grad_weights, axis=1, keepdims=True))
        ).astype(jnp.bfloat16)
        grad_query = product(grad_scores, k_head) * SCALE
        grad_key = contract(grad_scores, q_head, 0, 0) * SCALE
        grad_value = contract(weights.astype(jnp.bfloat16), g_head, 0, 0)
        return (grad_query, grad_key, grad_value)

    grad_query, grad_key, grad_value = lax.map(
        head_backward,
        (
            split_heads(queries),
            split_heads(back_keys),
            split_heads(back_values),
            split_heads(grad_attended),
            log_total,
        ),
    )
    grad_key, grad_value = (
        lax.psum_scatter(
            join_heads(grad_key).astype(jnp.bfloat16), "hidden", scatter_dimension=0, tiled=True
        ).astype(jnp.float32),
        lax.psum_scatter(
            join_heads(grad_value).astype(jnp.bfloat16), "hidden", scatter_dimension=0, tiled=True
        ).astype(jnp.float32),
    )
    grad_query = join_heads(grad_query).astype(jnp.bfloat16)
    grad_key = grad_key.astype(jnp.bfloat16)
    grad_value = grad_value.astype(jnp.bfloat16)
    query_grad = contract(h_one, grad_query, 0, 0)
    key_grad = contract(h_one, grad_key, 0, 0)
    value_grad = contract(h_one, grad_value, 0, 0)
    grad_h_one = (
        contract(grad_query, w_query, 1, 1)
        + contract(grad_key, w_key, 1, 1)
        + contract(grad_value, w_value, 1, 1)
    )
    gain_one_grad = jnp.sum(grad_h_one * normed_one, axis=0)
    shift_one_grad = jnp.sum(grad_h_one, axis=0)
    input_grad = (grad_residual + norm_back(grad_h_one, normed_one, inverse_one, gain_one)).astype(
        jnp.bfloat16
    )
    totals = lax.psum(
        (
            gain_one_grad,
            shift_one_grad,
            query_grad,
            key_grad,
            value_grad,
            out_proj_grad,
            gain_two_grad,
            shift_two_grad,
            router_grad,
            counts,
        ),
        ("expert", "hidden"),
    )
    total_tokens = row_count * lax.axis_size("expert") * lax.axis_size("hidden")
    load = totals[9] * experts / (total_tokens * top_count)
    return (
        output,
        input_grad,
        totals[0],
        totals[1],
        totals[2],
        totals[3],
        totals[4],
        totals[5],
        totals[6],
        totals[7],
        totals[8],
        up_grad,
        down_grad,
        load,
    )


def solution(mesh):
    in_specs = (
        P(("expert", "hidden"), None),
        P("expert", None),
        P(("expert", "hidden"), None),
        P(),
        P(),
        P(),
        P(),
        P(),
        P(),
        P(),
        P(),
        P(),
        P("expert", None, "hidden"),
        P("expert", "hidden", None),
        P(("expert", "hidden"), None),
    )
    out_specs = (
        P(("expert", "hidden"), None),
        P(("expert", "hidden"), None),
        P(),
        P(),
        P(),
        P(),
        P(),
        P(),
        P(),
        P(),
        P(),
        P("expert", None, "hidden"),
        P("expert", "hidden", None),
        P(),
    )
    return jax.shard_map(shards, mesh=mesh, in_specs=in_specs, out_specs=out_specs, check_vma=False)
```

profile of v0, /device:TPU:0, one launch (start us, length us, event | category | flops | bytes accessed | tf_op | source)
XLA Modules:
  0.0 1053.0 jit_solution(8360045255467511472)
XLA Ops:
  32.1 13.0 %all-gather.5.cloned.1.call-done = bf16[2048,768]{1,0:T(8,128)(2,1)} async-done(((bf16[512,768]{1,0:T(8,128)(2,1)}), bf16[2048,768]{1,0:T(8,128)(2,1)}) %all-gather.5.cloned.1.call-update) | async-done | bytes 3145744 | tf_op jit(solution)/shard_map/all_gather | solution.py:81
  56.6 19.4 %all-gather.7.cloned.1.call-done = bf16[2048,768]{1,0:T(8,128)(2,1)} async-done(((bf16[512,768]{1,0:T(8,128)(2,1)}), bf16[2048,768]{1,0:T(8,128)(2,1)}) %all-gather.7.cloned.1.call-update) | async-done | bytes 3145744 | tf_op jit(solution)/shard_map/all_gather | solution.py:82
  88.2 85.5 %while.28 = (s32[]{:T(128)}, bf16[12,512,64]{1,2,0:T(8,128)(2,1)}, f32[12,512]{1,0:T(8,128)}, bf16[12,512,64]{2,1,0:T(8,128)(2,1)S(1)}, bf16[12,2048,64]{2,1,0:T...) while((s32[]{:T(128)}, bf16[12,512,64]{1,2,0:T(8,128)(2,1)}, ...), condition=%wide.region_8.9_spmd.clone, body=%wide.region_5.8_spmd.clone.sunk | while | flops 279969280 | bytes 13928569 | solution.py:101
  181.0 7.7 scatter_custom_fusion
  188.8 51.8 %all_to_all.20 = bf16[8,160,768]{2,1,0:T(8,128)(2,1)} all-to-all(bf16[8,160,768]{2,1,0:T(8,128)(2,1)} %bitcast.191), channel_id=1, replica_groups=mesh['expert'=8,'hidden'=4] {'expert'}, dimensions={0} | all-to-all | bytes 3932160 | tf_op jit(solution)/shard_map/all_to_all | solution.py:126
  257.5 48.8 %all_to_all.21 = bf16[8,160,768]{2,1,0:T(8,128)(2,1)} all-to-all(bf16[8,160,768]{2,1,0:T(8,128)(2,1)S(1)} %bitcast.190), channel_id=1, replica_groups=mesh['expert'=8,'hidden'=4] {'expert'}, dimensions={0} | all-to-all | bytes 3932160 | tf_op jit(solution)/shard_map/all_to_all | solution.py:164
  306.6 12.8 %fusion.72 = f32[5120,768]{1,0:T(8,128)} fusion(bf16[5120,768]{1,0:T(8,128)(2,1)} %all-gather.9.cloned.1.call-done, bf16[1,768,768]{2,1,0:T(8,128)(2,1)S(1)} %copy-done), kind=kOutput, calls=%fused_computation.115 | convolution fusion | flops 6039797760 | bytes 24772608 | tf_op jit(solution)/shard_map/dot_general | solution.py:16
  319.4 40.1 %all-gather.11.cloned.1.call-done = bf16[5120,768]{1,0:T(8,128)(2,1)} async-done(((bf16[1280,768]{1,0:T(8,128)(2,1)}), bf16[5120,768]{1,0:T(8,128)(2,1)}) %all-gather.11.cloned.1.call-update) | async-done | bytes 7864336 | tf_op jit(solution)/shard_map/all_gather | solution.py:168
  359.5 19.0 %fusion.50 = bf16[5120,768]{1,0:T(8,128)(2,1)S(1)} fusion(f32[5120,768]{1,0:T(8,128)} %fusion.72, bf16[5120,768]{1,0:T(8,128)(2,1)} %all-gather.11.cloned.1.call-done, bf16[1,768,768]{2,1,0:T(8,128)(2,1)S(1)} %copy-done.40), kind=kOutput, calls=%fused_computation.67 | convolution fusion | flops 6118440960 | bytes 32636928 | tf_op jit(solution)/shard_map/dot_general | solution.py:20
  381.7 8.7 convolution_convert_fusion
  390.5 14.8 %convolution_convert_fusion.1 = bf16[5120,768]{1,0:T(8,128)(2,1)} fusion(bf16[1,768,768]{2,1,0:T(8,128)(2,1)S(1)} %copy-done.40, f32[5120,768]{1,0:T(8,128)} %fusion.72), kind=kOutput, calls=%fused_computation.70 | convolution fusion | flops 6079119360 | bytes 24772608 | tf_op jit(solution)/shard_map/dot_general | solution.py:16
  405.3 54.2 %reduce-scatter.7.cloned.1.call-done = bf16[1280,768]{1,0:T(8,128)(2,1)} async-done(((bf16[5120,768]{1,0:T(8,128)(2,1)}), bf16[1280,768]{1,0:T(8,128)(2,1)}) %reduce-scatter.7.cloned.1.call-update) | async-done | bytes 1966096 | tf_op jit(solution)/shard_map/reduce_scatter | solution.py:174
  465.0 66.1 %reduce-scatter.5.cloned.1.call-done = bf16[1280,768]{1,0:T(8,128)(2,1)} async-done(((bf16[5120,768]{1,0:T(8,128)(2,1)}), bf16[1280,768]{1,0:T(8,128)(2,1)}) %reduce-scatter.5.cloned.1.call-update) | async-done | bytes 1966096 | tf_op jit(solution)/shard_map/reduce_scatter | solution.py:133
  538.1 14.3 %gather_fusion.1 = bf16[1024,768]{1,0:T(8,128)(2,1)} fusion(bf16[8,160,768]{2,1,0:T(8,128)(2,1)S(1)} %all-to-all-done.3, s32[1024]{0:T(1024)S(1)} %bitcast.184), kind=kCustom, calls=%fused_computation.1 | custom fusion | bytes 3153920 | tf_op jit(solution)/shard_map/gather | solution.py:187
  557.3 25.0 %all-to-all-done.1 = bf16[8,160,768]{2,1,0:T(8,128)(2,1)} async-done(((bf16[8,160,768]{2,1,0:T(8,128)(2,1)}), bf16[8,160,768]{2,1,0:T(8,128)(2,1)}, u32[]{:S(2)}, u32[]{:S(2)}) %all-to-all-start.1) | async-done | bytes 1966112 | tf_op jit(solution)/shard_map/all_to_all | solution.py:136
  582.3 19.8 %gather_fusion = bf16[1024,768]{1,0:T(8,128)(2,1)} fusion(bf16[8,160,768]{2,1,0:T(8,128)(2,1)} %all-to-all-done.1, s32[1024]{0:T(1024)S(1)} %bitcast.185), kind=kCustom, calls=%fused_computation | custom fusion | bytes 3153920 | tf_op jit(solution)/shard_map/gather | solution.py:144
  605.6 9.5 multiply_reduce_fusion.1
  626.7 132.8 %while.29 = (s32[]{:T(128)}, bf16[12,512,64]{1,2,0:T(8,128)(2,1)S(1)}, bf16[12,2048,64]{1,2,0:T(8,128)(2,1)}, bf16[12,2048,64]{1,2,0:T(8,128)(2,1)}, bf16[12,512...) while((s32[]{:T(128)}, ...), condition=%wide.region_30.31_spmd.clone, body=%wide.region_28.30_spmd.clone.sunk | while | flops 683834880 | bytes 34630792 | solution.py:213
  766.8 28.9 %reduce-scatter.9.cloned.1.call-done = bf16[512,768]{0,1:T(8,128)(2,1)} async-done(((bf16[2048,768]{0,1:T(8,128)(2,1)}), bf16[512,768]{0,1:T(8,128)(2,1)}) %reduce-scatter.9.cloned.1.call-update) | async-done | bytes 786448 | tf_op jit(solution)/shard_map/reduce_scatter | solution.py:224
  799.3 37.1 %reduce-scatter.11.cloned.1.call-done = bf16[512,768]{0,1:T(8,128)(2,1)} async-done(((bf16[2048,768]{0,1:T(8,128)(2,1)}), bf16[512,768]{0,1:T(8,128)(2,1)}) %reduce-scatter.11.cloned.1.call-update) | async-done | bytes 786448 | tf_op jit(solution)/shard_map/reduce_scatter | solution.py:227
  840.0 12.2 %multiply_bitcast_fusion.1 = f32[1,768,768]{2,1,0:T(8,128)} fusion(bf16[5120,768]{1,0:T(8,128)(2,1)} %all-gather.9.cloned.1.call-done, bf16[5120,768]{1,0:T(8,128)(2,1)} %copy-done.48, f32[]{:T(128)S(6)} %convert_element_type.180), kind=kOutput, calls=%fused_computation.78 | convolution fusion | flops 6040387584 | bytes 18087940 | tf_op jit(solution)/shard_map/dot_general | solution.py:20
  852.2 14.4 %multiply_bitcast_fusion = f32[1,768,768]{2,1,0:T(8,128)} fusion(bf16[5120,768]{1,0:T(8,128)(2,1)} %all-gather.11.cloned.1.call-done, f32[]{:T(128)S(6)} %convert_element_type.180, f32[5120,768]{1,0:T(8,128)} %fusion.72), kind=kOutput, calls=%fused_computation.77 | convolution fusion | flops 6075777024 | bytes 25952260 | tf_op jit(solution)/shard_map/dot_general | solution.py:20
  872.6 41.3 %all-reduce = (f32[768]{0:T(1024)}, f32[768]{0:T(1024)}, f32[768]{0:T(1024)}, f32[768]{0:T(1024)}, f32[768,8]{0,1:T(8,128)}, /*index=5*/f32[8]{0:T(128)S(1)}) all-reduce(f32[768]{0:T(1024)S(1)} %get-tuple-element.230, f32[768]{0:T(1024)S(1)} %get-tuple-element.235, ...), channel_id=1, replica_groups=mesh['expert'=8,'hidden'=4] {'expert','hidden'}, use_global_device_ids=true, to_apply=%region_36.37 | all-reduce | flops 9224 | bytes 73792 | tf_op jit(solution)/shard_map/psum | solution.py:247
  917.3 119.2 %all-reduce.4.cloned.1.call-done = (f32[768,768]{1,0:T(8,128)}, f32[768,768]{1,0:T(8,128)}, f32[768,768]{1,0:T(8,128)}, f32[768,768]{1,0:T(8,128)}) async-done(((f32[768,768]{1,0:T(8,128)}, f32[768,768]{1,0:T(8,128)}, f32[768,768]{1,0:T(8,128)}, f32[768,768]{1,0:T(8,128)}), (f32[768,768]{1,0:T(8,128)}, f32[768,768]{1,0:T(8,128)}, f32[768,768]{1,0:T(8,128)}, ...) | async-done | bytes 9437200 | tf_op jit(solution)/shard_map/psum | solution.py:247
  (346 shorter events, 360.1 us)
Async XLA Ops:
  7.2 299.4 %copy-start = (bf16[1,768,768]{2,1,0:T(8,128)(2,1)S(1)}, bf16[1,768,768]{2,1,0:T(8,128)(2,1)}, u32[]{:S(2)}) copy-start(bf16[1,768,768]{2,1,0:T(8,128)(2,1)} %param.31) | copy-start | bytes 3538948
  7.2 37.9 %all-gather.5.cloned.1.call-start = ((), (), s32[]{:S(2)}) async-start(), calls=%async_computation.8 | async-start | bytes 3932160 | tf_op jit(solution)/shard_map/all_gather | solution.py:81
  8.6 12.4 %copy-start.26 = (f32[512]{0:T(512)}, f32[512]{0:T(512)S(1)}, u32[]{:S(2)}) copy-start(f32[512]{0:T(512)S(1)} %broadcast_multiply_fusion.5) | copy-start | bytes 6148
  10.2 10.9 %copy-start.30 = (f32[512]{0:T(512)}, f32[512]{0:T(512)S(1)}, u32[]{:S(2)}) copy-start(f32[512]{0:T(512)S(1)} %add_rsqrt_fusion.1) | copy-start | bytes 6148
  13.7 62.2 %all-gather.7.cloned.1.call-start = ((), (), s32[]{:S(2)}) async-start(), calls=%async_computation.9 | async-start | bytes 3932160 | tf_op jit(solution)/shard_map/all_gather | solution.py:82
  15.7 290.9 %all-gather.9.cloned.1.call-start = ((), (), s32[]{:S(2)}) async-start(), calls=%async_computation.10 | async-start | bytes 9830400 | tf_op jit(solution)/shard_map/all_gather | solution.py:129
  80.7 7.5 copy-start.35
  178.7 71.0 %copy-start.6 = (bf16[512,768]{1,0:T(8,128)(2,1)}, bf16[512,768]{1,0:T(8,128)(2,1)S(1)}, u32[]{:S(2)}) copy-start(bf16[512,768]{1,0:T(8,128)(2,1)S(1)} %add_convert_fusion.1) | copy-start | bytes 2359300
  240.6 118.9 %all-gather.11.cloned.1.call-start = ((), (), s32[]{:S(2)}) async-start(), calls=%async_computation.12 | async-start | bytes 9830400 | tf_op jit(solution)/shard_map/all_gather | solution.py:168
  244.2 5.5 copy-start.23
  306.3 53.2 %copy-start.40 = (bf16[1,768,768]{2,1,0:T(8,128)(2,1)S(1)}, bf16[1,768,768]{2,1,0:T(8,128)(2,1)}, u32[]{:S(2)}) copy-start(bf16[1,768,768]{2,1,0:T(8,128)(2,1)} %param.32) | copy-start | bytes 3538948
  306.3 153.2 %reduce-scatter.7.cloned.1.call-start = ((), (), s32[]{:S(2)}) async-start(), calls=%async_computation.13 | async-start | bytes 9830400 | tf_op jit(solution)/shard_map/reduce_scatter | solution.py:174
  390.4 140.7 %reduce-scatter.5.cloned.1.call-start = ((), (), s32[]{:S(2)}) async-start(), calls=%async_computation.11 | async-start | bytes 9830400 | tf_op jit(solution)/shard_map/reduce_scatter | solution.py:133
  459.5 71.6 %all-to-all-start.3 = ((bf16[8,160,768]{2,1,0:T(8,128)(2,1)}), bf16[8,160,768]{2,1,0:T(8,128)(2,1)S(1)}, u32[]{:S(2)}, u32[]{:S(2)}) async-start(bf16[8,160,768]{2,1,0:T(8,128)(2,1)} %bitcast.199), calls=%async_computation.5 | async-start | bytes 3932160 | tf_op jit(solution)/shard_map/all_to_all | solution.py:179
  531.1 5.7 copy-start.9
  531.1 51.2 %all-to-all-start.1 = ((bf16[8,160,768]{2,1,0:T(8,128)(2,1)}), bf16[8,160,768]{2,1,0:T(8,128)(2,1)}, u32[]{:S(2)}, u32[]{:S(2)}) async-start(bf16[8,160,768]{2,1,0:T(8,128)(2,1)} %bitcast.198), calls=%async_computation.2 | async-start | bytes 3932160 | tf_op jit(solution)/shard_map/all_to_all | solution.py:136
  536.8 258.9 %reduce-scatter.9.cloned.1.call-start = ((), (), s32[]{:S(2)}) async-start(), calls=%async_computation.14 | async-start | bytes 3932160 | tf_op jit(solution)/shard_map/reduce_scatter | solution.py:224
  616.3 5.7 copy-start.3
  616.3 5.8 copy-start.29
  759.6 76.8 %reduce-scatter.11.cloned.1.call-start = ((), (), s32[]{:S(2)}) async-start(), calls=%async_computation.15 | async-start | bytes 3932160 | tf_op jit(solution)/shard_map/reduce_scatter | solution.py:227
  760.4 276.1 %all-reduce.4.cloned.1.call-start = ((), (), s32[]{:S(2)}) async-start(), calls=%async_computation.16 | async-start | bytes 18874368 | tf_op jit(solution)/shard_map/psum | solution.py:247
  852.2 14.4 %copy-start.7 = (bf16[512,768]{1,0:T(8,128)(2,1)S(1)}, bf16[512,768]{1,0:T(8,128)(2,1)}, u32[]{:S(2)}) copy-start(bf16[512,768]{1,0:T(8,128)(2,1)} %copy-done.6) | copy-start | bytes 2359300
  852.2 14.8 %copy-start.21 = (bf16[12,512,64]{1,2,0:T(8,128)(2,1)S(1)}, bf16[12,512,64]{1,2,0:T(8,128)(2,1)}, u32[]{:S(2)}) copy-start(bf16[12,512,64]{1,2,0:T(8,128)(2,1)} %copy-done.20) | copy-start | bytes 2359300
  852.2 14.8 %copy-start.42 = (bf16[768,768]{1,0:T(8,128)(2,1)S(1)}, bf16[768,768]{1,0:T(8,128)(2,1)}, u32[]{:S(2)}) copy-start(bf16[768,768]{1,0:T(8,128)(2,1)} %param.24) | copy-start | bytes 3538948
  (36 other events, 83.2 us)
Sparse Core Ops, SparseCore 0:
  13.8 31.2 all-gather.4
  47.2 28.6 all-gather.6
  240.7 53.0 all-gather.8
  306.4 53.0 all-gather.10
  390.5 68.9 reduce-scatter.6
  462.1 68.9 reduce-scatter.4
  759.6 36.0 reduce-scatter.8
  798.4 37.9 reduce-scatter.10
  843.2 193.2 all-reduce.3
where the time goes:
time: 1060 us; the launch traced here: 1050 us
  waiting for transfers between devices  404 us (38%)
  matrix products  292 us (28%)
  blocking collectives  142 us (13%)
  local copies, waits for them, and re-layouts  134 us (13%)
  other arithmetic  54.7 us (5%)
  between operations  14.7 us (1%)
  starting transfers between devices  11.9 us (1%)
    dot_general x72, matrix products, contract(): lax.dot_general(left, right, (((left_axis,), (right_axis,)), ((), ())), p...  197 us
    psum x1, waiting for transfers between devices, shards(): lax.psum((gain_one_grad, shift_one_grad, query_grad, key_grad, value_grad...  119 us
    dot_general x30, matrix products, product(): return jnp.dot(left, right, preferred_element_type=jnp.float32)  92.8 us
    reduce_scatter x1, waiting for transfers between devices, shards(): lax.psum_scatter(partial_sum.astype(jnp.bfloat16), 'hidden', scatter_dime...  66.1 us
    reduce_scatter x1, waiting for transfers between devices, shards(): lax.psum_scatter(partial_in.astype(jnp.bfloat16), 'hidden', scatter_dimen...  54.2 us
    all_to_all x1, blocking collectives, shards(): lax.all_to_all(outgoing, 'expert', split_axis=0, concat_axis=0, tiled=True)  51.8 us
    all_to_all x1, blocking collectives, shards(): lax.all_to_all(grad_outgoing, 'expert', split_axis=0, concat_axis=0, tile...  48.8 us
    unnamed x107, local copies, waits for them, and re-layouts  41.6 us
  transfers between devices with their start and end apart: 11, of which 9 were waited for; matrix products, arithmetic and copies ran while one was open for 13% of the time, Pallas kernels for 0%

commit v1 on v0

--- a/solution.py
+++ b/solution.py
@@ -79,7 +79,10 @@
     value_proj = product(h_one, w_value).astype(jnp.bfloat16)
     all_keys, all_values = (
         lax.all_gather(key_proj, "hidden", axis=0, tiled=True),
-        lax.all_gather(value_proj, "hidden", axis=0, tiled=True),
+        jnp.concatenate(
+            lax.all_to_all(jnp.stack([value_proj] * lax.axis_size("hidden")), "hidden", 0, 0),
+            axis=0,
+        ),
     )
     key_count = all_keys.shape[0]
     doc_ends = jnp.cumsum(doc_lengths[0])

time: 1060 us -> 1080 us (1.019)
    all_to_all x0 -> x1, waiting for transfers between devices: none -> 37.2 us  [shards(): lax.all_to_all(jnp.stack([value_proj] * lax.axis_size('hidden')), 'hidden...]
    all_gather x1 -> x0, waiting for transfers between devices: 19.4 us -> none  [shards(): lax.all_gather(value_proj, 'hidden', axis=0, tiled=True)]
    all_gather x1, waiting for transfers between devices: 13 us -> 0.01 us  [shards(): lax.all_gather(key_proj, 'hidden', axis=0, tiled=True)]
  transfers between devices with their start and end apart: 11 -> 11, of which waited for: 9 -> 8; matrix products, arithmetic and copies ran while one was open for 13% -> 14% of each run, Pallas kernels for 0% -> 0%
where the time goes in v1:
time: 1080 us; the launch traced here: 1070 us
  waiting for transfers between devices  409 us (38%)
  matrix products  292 us (27%)
  local copies, waits for them, and re-layouts  144 us (13%)
  blocking collectives  142 us (13%)
  other arithmetic  54.7 us (5%)
  starting transfers between devices  16.6 us (2%)
  between operations  15 us (1%)
    dot_general x72, matrix products, contract(): lax.dot_general(left, right, (((left_axis,), (right_axis,)), ((), ())), p...  197 us
    psum x1, waiting for transfers between devices, shards(): lax.psum((gain_one_grad, shift_one_grad, query_grad, key_grad, value_grad...  119 us
    dot_general x30, matrix products, product(): return jnp.dot(left, right, preferred_element_type=jnp.float32)  93 us
    reduce_scatter x1, waiting for transfers between devices, shards(): lax.psum_scatter(partial_sum.astype(jnp.bfloat16), 'hidden', scatter_dime...  66.1 us
    reduce_scatter x1, waiting for transfers between devices, shards(): lax.psum_scatter(partial_in.astype(jnp.bfloat16), 'hidden', scatter_dimen...  54.2 us
    all_to_all x1, blocking collectives, shards(): lax.all_to_all(outgoing, 'expert', split_axis=0, concat_axis=0, tiled=True)  51.5 us
    all_to_all x1, blocking collectives, shards(): lax.all_to_all(grad_outgoing, 'expert', split_axis=0, concat_axis=0, tile...  48.8 us
    psum x1, blocking collectives, shards(): lax.psum((gain_one_grad, shift_one_grad, query_grad, key_grad, value_grad...  41.3 us
  transfers between devices with their start and end apart: 11, of which 8 were waited for; matrix products, arithmetic and copies ran while one was open for 14% of the time, Pallas kernels for 0%

profile of v1, /device:TPU:0, one launch (start us, length us, event | category | flops | bytes accessed | tf_op | source)
XLA Modules:
  0.0 1072.9 jit_solution(9123067136643722671)
XLA Ops:
  40.2 37.2 %all-to-all-done = bf16[4,512,768]{1,2,0:T(8,128)(2,1)} async-done(((bf16[4,512,768]{1,2,0:T(8,128)(2,1)}), bf16[4,512,768]{1,2,0:T(8,128)(2,1)}, u32[]{:S(2)}, u32[]{:S(2)}) %all-to-all-start) | async-done | bytes 3145760 | tf_op jit(solution)/shard_map/all_to_all | solution.py:83
  108.2 85.5 %while.28 = (s32[]{:T(128)}, bf16[12,512,64]{1,2,0:T(8,128)(2,1)}, f32[12,512]{1,0:T(8,128)}, bf16[12,512,64]{2,1,0:T(8,128)(2,1)S(1)}, bf16[12,2048,64]{2,1,0:T...) while((s32[]{:T(128)}, bf16[12,512,64]{1,2,0:T(8,128)(2,1)}, ...), condition=%wide.region_8.9_spmd.clone, body=%wide.region_5.8_spmd.clone.sunk | while | flops 279969280 | bytes 13928569 | solution.py:104
  201.1 7.4 scatter_custom_fusion
  208.5 51.5 %all_to_all.25 = bf16[8,160,768]{2,1,0:T(8,128)(2,1)} all-to-all(bf16[8,160,768]{2,1,0:T(8,128)(2,1)} %bitcast.191), channel_id=1, replica_groups=mesh['expert'=8,'hidden'=4] {'expert'}, dimensions={0} | all-to-all | bytes 3932160 | tf_op jit(solution)/shard_map/all_to_all | solution.py:129
  269.9 7.0 scatter_custom_fusion.1
  277.0 48.8 %all_to_all.26 = bf16[8,160,768]{2,1,0:T(8,128)(2,1)} all-to-all(bf16[8,160,768]{2,1,0:T(8,128)(2,1)S(1)} %bitcast.190), channel_id=1, replica_groups=mesh['expert'=8,'hidden'=4] {'expert'}, dimensions={0} | all-to-all | bytes 3932160 | tf_op jit(solution)/shard_map/all_to_all | solution.py:167
  325.9 13.0 %fusion.72 = f32[5120,768]{1,0:T(8,128)} fusion(bf16[5120,768]{1,0:T(8,128)(2,1)} %all-gather.6.cloned.1.call-done, bf16[1,768,768]{2,1,0:T(8,128)(2,1)S(1)} %copy-done), kind=kOutput, calls=%fused_computation.115 | convolution fusion | flops 6039797760 | bytes 24772608 | tf_op jit(solution)/shard_map/dot_general | solution.py:16
  338.9 40.1 %all-gather.8.cloned.1.call-done = bf16[5120,768]{1,0:T(8,128)(2,1)} async-done(((bf16[1280,768]{1,0:T(8,128)(2,1)}), bf16[5120,768]{1,0:T(8,128)(2,1)}) %all-gather.8.cloned.1.call-update) | async-done | bytes 7864336 | tf_op jit(solution)/shard_map/all_gather | solution.py:171
  379.0 19.0 %fusion.50 = bf16[5120,768]{1,0:T(8,128)(2,1)S(1)} fusion(f32[5120,768]{1,0:T(8,128)} %fusion.72, bf16[5120,768]{1,0:T(8,128)(2,1)} %all-gather.8.cloned.1.call-done, bf16[1,768,768]{2,1,0:T(8,128)(2,1)S(1)} %copy-done.40), kind=kOutput, calls=%fused_computation.67 | convolution fusion | flops 6118440960 | bytes 32636928 | tf_op jit(solution)/shard_map/dot_general | solution.py:20
  401.1 8.8 convolution_convert_fusion
  410.0 14.8 %convolution_convert_fusion.1 = bf16[5120,768]{1,0:T(8,128)(2,1)} fusion(bf16[1,768,768]{2,1,0:T(8,128)(2,1)S(1)} %copy-done.40, f32[5120,768]{1,0:T(8,128)} %fusion.72), kind=kOutput, calls=%fused_computation.70 | convolution fusion | flops 6079119360 | bytes 24772608 | tf_op jit(solution)/shard_map/dot_general | solution.py:16
  424.8 54.2 %reduce-scatter.7.cloned.1.call-done = bf16[1280,768]{1,0:T(8,128)(2,1)} async-done(((bf16[5120,768]{1,0:T(8,128)(2,1)}), bf16[1280,768]{1,0:T(8,128)(2,1)}) %reduce-scatter.7.cloned.1.call-update) | async-done | bytes 1966096 | tf_op jit(solution)/shard_map/reduce_scatter | solution.py:177
  484.6 66.1 %reduce-scatter.5.cloned.1.call-done = bf16[1280,768]{1,0:T(8,128)(2,1)} async-done(((bf16[5120,768]{1,0:T(8,128)(2,1)}), bf16[1280,768]{1,0:T(8,128)(2,1)}) %reduce-scatter.5.cloned.1.call-update) | async-done | bytes 1966096 | tf_op jit(solution)/shard_map/reduce_scatter | solution.py:136
  557.6 14.4 %gather_fusion.1 = bf16[1024,768]{1,0:T(8,128)(2,1)} fusion(bf16[8,160,768]{2,1,0:T(8,128)(2,1)S(1)} %all-to-all-done.4, s32[1024]{0:T(1024)S(1)} %bitcast.184), kind=kCustom, calls=%fused_computation.1 | custom fusion | bytes 3153920 | tf_op jit(solution)/shard_map/gather | solution.py:190
  576.8 25.0 %all-to-all-done.2 = bf16[8,160,768]{2,1,0:T(8,128)(2,1)} async-done(((bf16[8,160,768]{2,1,0:T(8,128)(2,1)}), bf16[8,160,768]{2,1,0:T(8,128)(2,1)}, u32[]{:S(2)}, u32[]{:S(2)}) %all-to-all-start.2) | async-done | bytes 1966112 | tf_op jit(solution)/shard_map/all_to_all | solution.py:139
  601.8 19.8 %gather_fusion = bf16[1024,768]{1,0:T(8,128)(2,1)} fusion(bf16[8,160,768]{2,1,0:T(8,128)(2,1)} %all-to-all-done.2, s32[1024]{0:T(1024)S(1)} %bitcast.185), kind=kCustom, calls=%fused_computation | custom fusion | bytes 3153920 | tf_op jit(solution)/shard_map/gather | solution.py:147
  625.1 9.5 multiply_reduce_fusion.1
  646.3 132.8 %while.29 = (s32[]{:T(128)}, bf16[12,512,64]{1,2,0:T(8,128)(2,1)S(1)}, bf16[12,2048,64]{1,2,0:T(8,128)(2,1)}, bf16[12,2048,64]{1,2,0:T(8,128)(2,1)}, bf16[12,512...) while((s32[]{:T(128)}, ...), condition=%wide.region_30.31_spmd.clone, body=%wide.region_28.30_spmd.clone.sunk | while | flops 683834880 | bytes 34630792 | solution.py:216
  786.4 28.9 %reduce-scatter.9.cloned.1.call-done = bf16[512,768]{0,1:T(8,128)(2,1)} async-done(((bf16[2048,768]{0,1:T(8,128)(2,1)}), bf16[512,768]{0,1:T(8,128)(2,1)}) %reduce-scatter.9.cloned.1.call-update) | async-done | bytes 786448 | tf_op jit(solution)/shard_map/reduce_scatter | solution.py:227
  818.9 37.1 %reduce-scatter.11.cloned.1.call-done = bf16[512,768]{0,1:T(8,128)(2,1)} async-done(((bf16[2048,768]{0,1:T(8,128)(2,1)}), bf16[512,768]{0,1:T(8,128)(2,1)}) %reduce-scatter.11.cloned.1.call-update) | async-done | bytes 786448 | tf_op jit(solution)/shard_map/reduce_scatter | solution.py:230
  859.6 12.2 %multiply_bitcast_fusion.1 = f32[1,768,768]{2,1,0:T(8,128)} fusion(bf16[5120,768]{1,0:T(8,128)(2,1)} %all-gather.6.cloned.1.call-done, bf16[5120,768]{1,0:T(8,128)(2,1)} %copy-done.48, f32[]{:T(128)S(6)} %convert_element_type.180), kind=kOutput, calls=%fused_computation.78 | convolution fusion | flops 6040387584 | bytes 18087940 | tf_op jit(solution)/shard_map/dot_general | solution.py:20
  871.8 14.4 %multiply_bitcast_fusion = f32[1,768,768]{2,1,0:T(8,128)} fusion(bf16[5120,768]{1,0:T(8,128)(2,1)} %all-gather.8.cloned.1.call-done, f32[]{:T(128)S(6)} %convert_element_type.180, f32[5120,768]{1,0:T(8,128)} %fusion.72), kind=kOutput, calls=%fused_computation.77 | convolution fusion | flops 6075777024 | bytes 25952260 | tf_op jit(solution)/shard_map/dot_general | solution.py:20
  892.2 41.3 %all-reduce = (f32[768]{0:T(1024)}, f32[768]{0:T(1024)}, f32[768]{0:T(1024)}, f32[768]{0:T(1024)}, f32[768,8]{0,1:T(8,128)}, /*index=5*/f32[8]{0:T(128)S(1)}) all-reduce(f32[768]{0:T(1024)S(1)} %get-tuple-element.251, f32[768]{0:T(1024)S(1)} %get-tuple-element.256, ...), channel_id=1, replica_groups=mesh['expert'=8,'hidden'=4] {'expert','hidden'}, use_global_device_ids=true, to_apply=%region_36.37 | all-reduce | flops 9224 | bytes 73792 | tf_op jit(solution)/shard_map/psum | solution.py:250
  936.8 119.2 %all-reduce.4.cloned.1.call-done = (f32[768,768]{1,0:T(8,128)}, f32[768,768]{1,0:T(8,128)}, f32[768,768]{1,0:T(8,128)}, f32[768,768]{1,0:T(8,128)}) async-done(((f32[768,768]{1,0:T(8,128)}, f32[768,768]{1,0:T(8,128)}, f32[768,768]{1,0:T(8,128)}, f32[768,768]{1,0:T(8,128)}), (f32[768,768]{1,0:T(8,128)}, f32[768,768]{1,0:T(8,128)}, f32[768,768]{1,0:T(8,128)}, ...) | async-done | bytes 9437200 | tf_op jit(solution)/shard_map/psum | solution.py:250
  (348 shorter events, 368.2 us)
Async XLA Ops:
  7.2 318.7 %copy-start = (bf16[1,768,768]{2,1,0:T(8,128)(2,1)S(1)}, bf16[1,768,768]{2,1,0:T(8,128)(2,1)}, u32[]{:S(2)}) copy-start(bf16[1,768,768]{2,1,0:T(8,128)(2,1)} %param.31) | copy-start | bytes 3538948
  7.2 88.8 %all-gather.4.cloned.1.call-start = ((), (), s32[]{:S(2)}) async-start(), calls=%async_computation.9 | async-start | bytes 3932160 | tf_op jit(solution)/shard_map/all_gather | solution.py:81
  8.6 20.6 %copy-start.26 = (f32[512]{0:T(512)}, f32[512]{0:T(512)S(1)}, u32[]{:S(2)}) copy-start(f32[512]{0:T(512)S(1)} %broadcast_multiply_fusion.5) | copy-start | bytes 6148
  10.2 19.1 %copy-start.30 = (f32[512]{0:T(512)}, f32[512]{0:T(512)S(1)}, u32[]{:S(2)}) copy-start(f32[512]{0:T(512)S(1)} %add_rsqrt_fusion.1) | copy-start | bytes 6148
  18.9 6.6 copy-start.47
  18.9 58.4 %all-to-all-start = ((bf16[4,512,768]{1,2,0:T(8,128)(2,1)}), bf16[4,512,768]{1,2,0:T(8,128)(2,1)}, u32[]{:S(2)}, u32[]{:S(2)}) async-start(bf16[4,512,768]{1,2,0:T(8,128)(2,1)} %stack.2), calls=%async_computation | async-start | bytes 6291456 | tf_op jit(solution)/shard_map/all_to_all | solution.py:83
  23.7 302.2 %all-gather.6.cloned.1.call-start = ((), (), s32[]{:S(2)}) async-start(), calls=%async_computation.10 | async-start | bytes 9830400 | tf_op jit(solution)/shard_map/all_gather | solution.py:132
  100.8 7.5 copy-start.35
  198.8 70.4 %copy-start.6 = (bf16[512,768]{1,0:T(8,128)(2,1)}, bf16[512,768]{1,0:T(8,128)(2,1)S(1)}, u32[]{:S(2)}) copy-start(bf16[512,768]{1,0:T(8,128)(2,1)S(1)} %add_convert_fusion.1) | copy-start | bytes 2359300
  260.1 118.9 %all-gather.8.cloned.1.call-start = ((), (), s32[]{:S(2)}) async-start(), calls=%async_computation.12 | async-start | bytes 9830400 | tf_op jit(solution)/shard_map/all_gather | solution.py:171
  325.8 53.2 %copy-start.40 = (bf16[1,768,768]{2,1,0:T(8,128)(2,1)S(1)}, bf16[1,768,768]{2,1,0:T(8,128)(2,1)}, u32[]{:S(2)}) copy-start(bf16[1,768,768]{2,1,0:T(8,128)(2,1)} %param.32) | copy-start | bytes 3538948
  325.8 153.3 %reduce-scatter.7.cloned.1.call-start = ((), (), s32[]{:S(2)}) async-start(), calls=%async_computation.13 | async-start | bytes 9830400 | tf_op jit(solution)/shard_map/reduce_scatter | solution.py:177
  409.9 140.7 %reduce-scatter.5.cloned.1.call-start = ((), (), s32[]{:S(2)}) async-start(), calls=%async_computation.11 | async-start | bytes 9830400 | tf_op jit(solution)/shard_map/reduce_scatter | solution.py:136
  479.1 71.6 %all-to-all-start.4 = ((bf16[8,160,768]{2,1,0:T(8,128)(2,1)}), bf16[8,160,768]{2,1,0:T(8,128)(2,1)S(1)}, u32[]{:S(2)}, u32[]{:S(2)}) async-start(bf16[8,160,768]{2,1,0:T(8,128)(2,1)} %bitcast.199), calls=%async_computation.6 | async-start | bytes 3932160 | tf_op jit(solution)/shard_map/all_to_all | solution.py:182
  550.6 5.7 copy-start.9
  550.6 51.2 %all-to-all-start.2 = ((bf16[8,160,768]{2,1,0:T(8,128)(2,1)}), bf16[8,160,768]{2,1,0:T(8,128)(2,1)}, u32[]{:S(2)}, u32[]{:S(2)}) async-start(bf16[8,160,768]{2,1,0:T(8,128)(2,1)} %bitcast.198), calls=%async_computation.3 | async-start | bytes 3932160 | tf_op jit(solution)/shard_map/all_to_all | solution.py:139
  556.3 259.0 %reduce-scatter.9.cloned.1.call-start = ((), (), s32[]{:S(2)}) async-start(), calls=%async_computation.14 | async-start | bytes 3932160 | tf_op jit(solution)/shard_map/reduce_scatter | solution.py:227
  635.9 5.7 copy-start.3
  635.9 5.8 copy-start.29
  779.1 76.8 %reduce-scatter.11.cloned.1.call-start = ((), (), s32[]{:S(2)}) async-start(), calls=%async_computation.15 | async-start | bytes 3932160 | tf_op jit(solution)/shard_map/reduce_scatter | solution.py:230
  780.0 276.1 %all-reduce.4.cloned.1.call-start = ((), (), s32[]{:S(2)}) async-start(), calls=%async_computation.16 | async-start | bytes 18874368 | tf_op jit(solution)/shard_map/psum | solution.py:250
  871.8 14.4 %copy-start.7 = (bf16[512,768]{1,0:T(8,128)(2,1)S(1)}, bf16[512,768]{1,0:T(8,128)(2,1)}, u32[]{:S(2)}) copy-start(bf16[512,768]{1,0:T(8,128)(2,1)} %copy-done.6) | copy-start | bytes 2359300
  871.8 14.8 %copy-start.21 = (bf16[12,512,64]{1,2,0:T(8,128)(2,1)S(1)}, bf16[12,512,64]{1,2,0:T(8,128)(2,1)}, u32[]{:S(2)}) copy-start(bf16[12,512,64]{1,2,0:T(8,128)(2,1)} %copy-done.20) | copy-start | bytes 2359300
  871.8 14.8 %copy-start.42 = (bf16[768,768]{1,0:T(8,128)(2,1)S(1)}, bf16[768,768]{1,0:T(8,128)(2,1)}, u32[]{:S(2)}) copy-start(bf16[768,768]{1,0:T(8,128)(2,1)} %param.24) | copy-start | bytes 3538948
  (36 other events, 87.8 us)
Sparse Core Ops, SparseCore 0:
  13.8 47.3 all-gather.3
  260.2 53.1 all-gather.5
  325.9 53.0 all-gather.7
  410.0 68.9 reduce-scatter.6
  481.6 68.9 reduce-scatter.4
  779.2 36.0 reduce-scatter.8
  818.0 37.9 reduce-scatter.10
  862.7 193.2 all-reduce.3
